TPU v7x, 32 devices: a whole 2x2x4 slice. The times are simulated.
32 devices in a mesh: band: 8 (over z, core), blk: 4 (over y, x).
Axes of the slice: x: 2, y: 2, z: 4, core: 2. Of those that a mesh axis runs over, the one named last changes fastest.
Arguments:
- steering: bfloat16 [4, 6144, 512], P('blk', 'band'), may hold values from -1.4 to 1.4
- estimates: bfloat16 [4, 6144], P('blk', 'band'), may hold values from 0 to 1
- spectra: float32 [4, 256, 512], P('blk', 'band'), may hold values from -768 to 4160
Outputs:
- updated: float32 [4, 6144], P('blk', 'band')
- broadband: float32 [6144], P('band')
All inputs are finite; a program needn't handle non-finite values.
Results may differ from a plain program's by a relative error of at most 0.0003.
Values may be sent and summed in bfloat16 or wider, within the bound.
A program may use at most 192 MiB of HBM per device.

v0:
```python
import jax
import jax.numpy as jnp
from jax import lax
from jax.sharding import PartitionSpec as P

CHANNELS = 256


def body(steering, estimates, spectra):
    width = CHANNELS
    steer_wide = steering.astype(jnp.float32)
    turned = jnp.concatenate([-steering[..., width:], steering[..., :width]], axis=2)
    mine_values = estimates.astype(jnp.float32)
    piece = lax.all_gather(spectra, "band", axis=1, tiled=True)
    cross_real = piece[..., :width]
    cross_imag = piece[..., width:]
    kernel_real = jnp.concatenate([cross_real, -cross_imag], axis=2)
    kernel_imag = jnp.concatenate([cross_imag, cross_real], axis=2)
    real_part = jnp.einsum(
        "bgk,brk->bgr",
        steer_wide,
        kernel_real,
        precision=lax.Precision.HIGHEST,
        preferred_element_type=jnp.float32,
    )
    imag_part = jnp.einsum(
        "bgk,brk->bgr",
        steer_wide,
        kernel_imag,
        precision=lax.Precision.HIGHEST,
        preferred_element_type=jnp.float32,
    )
    count = piece.shape[1]
    weight_real = lax.slice_in_dim(steer_wide, 0, count, axis=2)
    weight_imag = lax.dynamic_slice_in_dim(steer_wide, width, count, 2)
    beam = jnp.sum(weight_real * real_part + weight_imag * imag_part, axis=2) / (width * width)
    blocks = lax.all_gather(steering, "band", axis=1, tiled=True)
    values = lax.all_gather(estimates, "band", axis=1, tiled=True)
    real_sum = jnp.einsum("bgk,bhk->bgh", steering, blocks, preferred_element_type=jnp.float32)
    imag_sum = jnp.einsum("bgk,bhk->bgh", turned, blocks, preferred_element_type=jnp.float32)
    tile = (real_sum * real_sum + imag_sum * imag_sum) / (width * width)
    applied = jnp.einsum(
        "bgh,bh->bg",
        tile,
        values.astype(jnp.float32),
        precision=lax.Precision.HIGHEST,
        preferred_element_type=jnp.float32,
    )
    power = jnp.sum(steer_wide * steer_wide, axis=2)
    diag = power * power / (width * width)
    updated = jnp.maximum(mine_values + (beam - applied) / diag, 0.0)
    broadband = lax.psum(jnp.sum(updated, axis=0), "blk")
    return (updated, broadband)


def solution(mesh):
    return jax.shard_map(
        body,
        mesh=mesh,
        in_specs=(P("blk", "band", None), P("blk", "band"), P("blk", "band", None)),
        out_specs=(P("blk", "band"), P("band")),
        check_vma=False,
    )
```

profile of v0, /device:TPU:0, one launch (start us, length us, event | category | flops | bytes accessed | tf_op | source)
XLA Modules:
  0.0 137.5 jit_solution(16953506634375215782)
XLA Ops:
  7.2 0.0 copy-start
  7.2 0.0 all-gather.2.cloned.1.call-start
  7.2 0.7 all-gather.2.cloned.1.call-update
  7.9 1.4 %copy.5 = bf16[1,768,512]{1,2,0:T(8,128)(2,1)S(1)} copy(bf16[1,768,512]{2,1,0:T(8,128)(2,1)} %param.3) | data formatting | bytes 1572864 | tf_op args[0]
  9.3 0.1 convert_element_type.8
  9.4 15.8 %all_gather.11 = bf16[1,6144]{1,0:T(2,128)(2,1)S(1)} all-gather(bf16[1,768]{1,0:T(2,128)(2,1)} %param.4), channel_id=1, replica_groups=mesh['band'=8,'blk'=4] {'band'}, dimensions={1}, use_global_device_ids=true | all-gather | bytes 13824 | tf_op jit(solution)/shard_map/all_gather | solution.py:38
  25.2 0.2 multiply_reduce_fusion
  25.4 18.2 %all_gather.9 = f32[1,256,512]{2,1,0:T(8,128)S(1)} all-gather(f32[1,32,512]{2,1,0:T(8,128)} %param.5), channel_id=1, replica_groups=mesh['band'=8,'blk'=4] {'band'}, dimensions={1}, use_global_device_ids=true | all-gather | bytes 589824 | tf_op jit(solution)/shard_map/all_gather | solution.py:14
  43.6 0.1 slice_negate_fusion.1
  43.7 0.0 copy-done
  43.7 0.8 fusion.12
  44.5 0.8 fusion.13
  45.4 0.1 slice_negate_fusion
  45.4 35.8 %all-gather.2.cloned.1.call-done = bf16[1,6144,512]{2,1,0:T(8,128)(2,1)} async-done(((bf16[1,768,512]{2,1,0:T(8,128)(2,1)}), bf16[1,6144,512]{2,1,0:T(8,128)(2,1)}) %all-gather.2.cloned.1.call-update) | async-done | bytes 6291472 | tf_op jit(solution)/shard_map/all_gather | solution.py:37
  81.2 0.0 copy-start.2
  81.2 12.0 %fusion.8 = f32[768,6144]{1,0:T(8,128)} fusion(bf16[1,6144,512]{2,1,0:T(8,128)(2,1)} %all-gather.2.cloned.1.call-done, bf16[1,768,512]{2,1,0:T(8,128)(2,1)S(1)} %copy-done), kind=kOutput, calls=%fused_computation.8 | convolution fusion | flops 4831838208 | bytes 25952256 | tf_op jit(solution)/shard_map/bgk,bhk->bgh/dot_general | solution.py:39
  93.2 0.0 copy-done.2
  93.2 9.0 %fusion.6 = f32[768,6144]{1,0:T(8,128)} fusion(bf16[1,6144,512]{2,1,0:T(8,128)(2,1)S(1)} %copy-done.2, bf16[1,768,256]{2,1,0:T(8,128)(2,1)S(1)} %get-tuple-element.5, bf16[1,768,256]{2,1,0:T(8,128)(2,1)S(1)} %get-tuple-element.4), kind=kOutput, calls=%fused_computation.6 | convolution fusion | flops 4833411072 | bytes 25952256 | tf_op jit(solution)/shard_map/bgk,bhk->bgh/dot_general | solution.py:40
  102.3 0.0 copy-start.1
  102.3 17.4 %fusion.14 = f32[768]{0:T(1024)S(1)} fusion(f32[768,6144]{1,0:T(8,128)} %fusion.6, f32[768,6144]{1,0:T(8,128)} %fusion.8, bf16[1,6144]{1,0:T(2,128)(2,1)S(1)} %all_gather.11), kind=kOutput, calls=%fused_computation.17 | convolution fusion | flops 75497472 | bytes 37764096 | tf_op jit(solution)/shard_map/bgh,bh->bg/dot_general | solution.py:42
  119.7 0.0 copy-done.1
  119.7 0.6 fusion.31
  120.3 10.4 %psum.7 = f32[768]{0:T(1024)} all-reduce(f32[768]{0:T(1024)S(1)} %get-tuple-element.2), channel_id=1, replica_groups=mesh['band'=8,'blk'=4] {'blk'}, use_global_device_ids=true, to_apply=%region_2.0 | all-reduce | flops 768 | bytes 6144 | tf_op jit(solution)/shard_map/psum | solution.py:52
  (1 shorter events, 0.0 us)
Async XLA Ops:
  7.2 36.5 %copy-start = (bf16[1,768,512]{2,1,0:T(8,128)(2,1)S(1)}, bf16[1,768,512]{2,1,0:T(8,128)(2,1)}, u32[]{:S(2)}) copy-start(bf16[1,768,512]{2,1,0:T(8,128)(2,1)} %param.3) | copy-start | bytes 2359300
  7.2 74.0 %all-gather.2.cloned.1.call-start = ((), (), s32[]{:S(2)}) async-start(), calls=%async_computation | async-start | bytes 7077888 | tf_op jit(solution)/shard_map/all_gather | solution.py:37
  81.2 12.1 %copy-start.2 = (bf16[1,6144,512]{2,1,0:T(8,128)(2,1)S(1)}, bf16[1,6144,512]{2,1,0:T(8,128)(2,1)}, u32[]{:S(2)}) copy-start(bf16[1,6144,512]{2,1,0:T(8,128)(2,1)} %all-gather.2.cloned.1.call-done) | copy-start | bytes 18874372
  102.3 17.4 %copy-start.1 = (bf16[1,768]{1,0:T(2,128)(2,1)S(1)}, bf16[1,768]{1,0:T(2,128)(2,1)}, u32[]{:S(2)}) copy-start(bf16[1,768]{1,0:T(2,128)(2,1)} %param.4) | copy-start | bytes 4612
Sparse Core Ops, SparseCore 0:
  9.6 71.5 all-gather.1
where the time goes:
time: 138 us
  blocking collectives  44.4 us (32%)
  matrix products  40.1 us (29%)
  waiting for transfers between devices  36.5 us (26%)
  between operations  14.1 us (10%)
  local copies, waits for them, and re-layouts  1.42 us (1%)
    all_gather x1, waiting for transfers between devices, body(): blocks = lax.all_gather(steering, 'band', axis=1, tiled=True)  35.8 us
    all_gather x1, blocking collectives, body(): piece = lax.all_gather(spectra, 'band', axis=1, tiled=True)  18.2 us
    dot_general x1, matrix products, body(): jnp.einsum('bgh,bh->bg', tile, values.astype(jnp.float32), precision=lax....  17.4 us
    all_gather x1, blocking collectives, body(): values = lax.all_gather(estimates, 'band', axis=1, tiled=True)  15.8 us
    dot_general x1, matrix products, body(): jnp.einsum('bgk,bhk->bgh', steering, blocks, preferred_element_type=jnp.f...  12 us
    psum x1, blocking collectives, body(): broadband = lax.psum(jnp.sum(updated, axis=0), 'blk')  10.4 us
    dot_general x1, matrix products, body(): jnp.einsum('bgk,bhk->bgh', turned, blocks, preferred_element_type=jnp.flo...  9.02 us
  transfers between devices with their start and end apart: 1, of which 1 were waited for; matrix products, arithmetic and copies ran while one was open for 3% of the time, Pallas kernels for 0%

commit v1 on v0

v1 whole, which is shorter than its diff:
```python
import functools

import jax
import jax.numpy as jnp
from jax import lax
from jax.experimental import pallas as pl
from jax.experimental.pallas import tpu as pltpu
from jax.sharding import PartitionSpec as P

MESH = pl.DeviceIdType.MESH
F32 = jnp.float32
BF16 = jnp.bfloat16


def split(value):
    high = value.astype(BF16)
    low = (value - high.astype(F32)).astype(BF16)
    return jnp.concatenate([high, low], axis=0)


def kernel(
    n, nb, s_ref, x_ref, c_ref, up_ref, bb_ref, t_ref, z_ref, a_ref, b_ref, pair_ref, mine_ref, part_ref, block_ref, d_ref, blk_ref,
    pair_send, pair_recv, part_send, part_recv, ring_send, ring_recv, over_send, over_recv, blk_send, blk_recv,
):
    me, group = lax.axis_index("band"), lax.axis_index("blk")
    chips = n // 2
    chip, core = me // 2, me % 2
    partner = chip * 2 + (1 - core)
    rows, width = c_ref.shape[0], c_ref.shape[1] // 2
    half = width // 2
    piece = half // chips
    others = [(chip + step) % chips for step in range(1, chips)]
    peers = [(group + step) % nb for step in range(1, nb)]

    barrier = pltpu.get_barrier_semaphore()
    pl.semaphore_signal(barrier, inc=1, device_id={"band": partner}, device_id_type=MESH)
    for other in others:
        pl.semaphore_signal(barrier, inc=1, device_id={"band": other * 2 + core}, device_id_type=MESH)
    for peer in peers:
        pl.semaphore_signal(barrier, inc=1, device_id={"blk": peer}, device_id_type=MESH)

    real, imag = c_ref[:, :width], c_ref[:, width:]
    t_ref[...] = jnp.zeros_like(t_ref)
    z_ref[...] = jnp.zeros_like(z_ref)
    within = pl.multiple_of((me % chips) * rows, rows)
    z_ref[pl.ds(within, rows), :] = (real + imag) * 0.5
    t_ref[:, pl.ds(pl.multiple_of((me // chips) * half, half), half)] = z_ref[...].T
    t_ref[pl.ds(pl.multiple_of(me * rows, rows), rows), :] += (real - imag) * 0.5

    x = x_ref[...].astype(F32)

    def build(side):
        at = pl.multiple_of(side * half, half)
        a_half = s_ref[:, pl.ds(at, half)].T
        b_half = s_ref[:, pl.ds(pl.multiple_of(width + side * half, half), half)].T
        a_ref[pl.ds(at, half), :] = a_half
        b_ref[pl.ds(at, half), :] = b_half
        a_wide, b_wide = a_half.astype(F32), b_half.astype(F32)
        total = jnp.dot(split(x * (a_wide - b_wide)), s_ref[:, :width], preferred_element_type=F32)
        total += jnp.dot(split(x * (a_wide + b_wide)), s_ref[:, width:], preferred_element_type=F32)
        return t_ref[pl.ds(at, half), :] - (total[:half] + total[half:])

    theirs = pl.multiple_of((1 - core) * half, half)
    t_ref[pl.ds(theirs, half), :] = build(1 - core)
    pl.semaphore_wait(barrier, 1 + len(others) + len(peers))
    swap = pltpu.make_async_remote_copy(
        src_ref=t_ref.at[pl.ds(theirs, half), :],
        dst_ref=pair_ref,
        send_sem=pair_send,
        recv_sem=pair_recv,
        device_id={"band": partner},
        device_id_type=MESH,
    )
    swap.start()
    own = build(core)
    swap.wait_recv()
    mine_ref[...] = (own + pair_ref[...]).reshape(mine_ref.shape)

    sends = []
    for step, other in enumerate(others):
        copy = pltpu.make_async_remote_copy(
            src_ref=mine_ref.at[other],
            dst_ref=part_ref.at[step],
            send_sem=part_send.at[step],
            recv_sem=part_recv.at[step],
            device_id={"band": other * 2 + core},
            device_id_type=MESH,
        )
        copy.start()
        sends.append(copy)

    a_wide, b_wide = a_ref[...].astype(F32), b_ref[...].astype(F32)
    power = jnp.sum(a_wide * a_wide + b_wide * b_wide, axis=0, keepdims=True)
    swap.wait_send()

    total = mine_ref[chip]
    for step in range(chips - 1):
        sends[step].wait_recv()
        total += part_ref[step]
    block_ref[...] = total

    def place(which, side):
        return pl.ds(pl.multiple_of(side * half + which * piece, piece), piece)

    gathers, handed = [], []

    def hand_over(index, source, which):
        copy = pltpu.make_async_remote_copy(
            src_ref=source,
            dst_ref=d_ref.at[place(which, core), :],
            send_sem=over_send.at[index],
            recv_sem=over_recv.at[index],
            device_id={"band": partner},
            device_id_type=MESH,
        )
        copy.start()
        handed.append(copy)

    for step, other in enumerate(others):
        copy = pltpu.make_async_remote_copy(
            src_ref=block_ref,
            dst_ref=d_ref.at[place(chip, core), :],
            send_sem=ring_send.at[step],
            recv_sem=ring_recv.at[step],
            device_id={"band": other * 2 + core},
            device_id_type=MESH,
        )
        copy.start()
        gathers.append(copy)
    hand_over(chips - 1, block_ref, chip)
    d_ref[place(chip, core), :] = total
    for step in range(chips - 1):
        gathers[step].wait_recv()
        source = (chip + chips - 1 - step) % chips
        hand_over(step, d_ref.at[place(source, core), :], source)
    for copy in handed:
        copy.wait_recv()

    d = split(d_ref[...])
    u = jnp.dot(d, a_ref[...], preferred_element_type=F32)
    v = jnp.dot(d, b_ref[...], preferred_element_type=F32)
    u, v = u[:width] + u[width:], v[:width] + v[width:]
    residual = jnp.sum(u * (a_wide - b_wide) + v * (a_wide + b_wide), axis=0, keepdims=True) / (width * width)
    updated = jnp.maximum(x + residual / (power * power / (width * width)), 0.0)
    up_ref[...] = updated
    blk_ref[group] = updated

    exchanges = []
    for step, peer in enumerate(peers):
        copy = pltpu.make_async_remote_copy(
            src_ref=blk_ref.at[group],
            dst_ref=blk_ref.at[group],
            send_sem=blk_send.at[step],
            recv_sem=blk_recv.at[step],
            device_id={"blk": peer},
            device_id_type=MESH,
        )
        copy.start()
        exchanges.append(copy)
    for copy in sends + gathers + handed:
        copy.wait_send()
    for copy in exchanges:
        copy.wait_recv()
    broad = blk_ref[0]
    for index in range(1, nb):
        broad += blk_ref[index]
    bb_ref[...] = broad
    for copy in exchanges:
        copy.wait_send()


def body(n, nb, steering, estimates, spectra):
    points, doubled = steering.shape[1:]
    width = doubled // 2
    chips, half = n // 2, width // 2
    dma = pltpu.SemaphoreType.DMA
    updated, broadband = pl.pallas_call(
        functools.partial(kernel, n, nb),
        out_shape=[jax.ShapeDtypeStruct((1, points), F32), jax.ShapeDtypeStruct((1, points), F32)],
        in_specs=[pl.BlockSpec(memory_space=pltpu.VMEM)] * 3,
        out_specs=[pl.BlockSpec(memory_space=pltpu.VMEM)] * 2,
        scratch_shapes=[
            pltpu.VMEM((width, width), F32),
            pltpu.VMEM((half, width), F32),
            pltpu.VMEM((width, points), BF16),
            pltpu.VMEM((width, points), BF16),
            pltpu.VMEM((half, width), F32),
            pltpu.VMEM((chips, half // chips, width), F32),
            pltpu.VMEM((chips - 1, half // chips, width), F32),
            pltpu.VMEM((half // chips, width), F32),
            pltpu.VMEM((width, width), F32),
            pltpu.VMEM((nb, 1, points), F32),
            dma, dma,
            dma((chips - 1,)), dma((chips - 1,)),
            dma((chips - 1,)), dma((chips - 1,)),
            dma((chips,)), dma((chips,)),
            dma((nb - 1,)), dma((nb - 1,)),
        ],
        compiler_params=pltpu.CompilerParams(collective_id=0, has_side_effects=True),
    )(steering[0], estimates, spectra[0])
    return updated, broadband.reshape(points)


def solution(mesh):
    return jax.shard_map(
        functools.partial(body, mesh.shape["band"], mesh.shape["blk"]),
        mesh=mesh,
        in_specs=(P("blk", "band", None), P("blk", "band"), P("blk", "band", None)),
        out_specs=(P("blk", "band"), P("band")),
        check_vma=False,
    )
```

time: 138 us -> 24.7 us (0.18)
  blocking collectives: 44.4 us -> 0 us
  matrix products: 40.1 us -> 0 us
  waiting for transfers between devices: 36.5 us -> 0 us
  Pallas kernels: 0 us -> 22 us
  between operations: 14.1 us -> 0.65 us
    dot_general x5 -> x0, matrix products: 40.1 us -> none  [the longest x1 17.4 us: body(): jnp.einsum('bgh,bh->bg', tile, values.astype(jnp.float32), precision=lax....]
    all_gather x1 -> x0, waiting for transfers between devices: 35.8 us -> none  [body(): blocks = lax.all_gather(steering, 'band', axis=1, tiled=True)]
    all_gather x2 -> x0, blocking collectives: 34 us -> none  [the longest x1 18.2 us: body(): piece = lax.all_gather(spectra, 'band', axis=1, tiled=True)]
    pallas_call x0 -> x1, Pallas kernels: none -> 22 us  [body(): pl.pallas_call(functools.partial(kernel, n, nb), out_shape=[jax.ShapeDtyp...]
    psum x1 -> x0, blocking collectives: 10.4 us -> none  [body(): broadband = lax.psum(jnp.sum(updated, axis=0), 'blk')]
  transfers between devices with their start and end apart: 1 -> 0, of which waited for: 1 -> 0; matrix products, arithmetic and copies ran while one was open for 3% -> 0% of each run, Pallas kernels for 0% -> 0%
where the time goes in v1:
time: 24.7 us; the launch traced here: 24.5 us
  Pallas kernels  22 us (89%)
  local copies, waits for them, and re-layouts  1.3 us (5%)
  between operations  0.65 us (3%)
  other arithmetic  0.6 us (2%)
    pallas_call x1, Pallas kernels, body(): pl.pallas_call(functools.partial(kernel, n, nb), out_shape=[jax.ShapeDtyp...  22 us
    unnamed x5, local copies, waits for them, and re-layouts  1.3 us
    pallas_call x1, other arithmetic, body(): pl.pallas_call(functools.partial(kernel, n, nb), out_shape=[jax.ShapeDtyp...  0.6 us

profile of v1, /device:TPU:0, one launch (start us, length us, event | category | flops | bytes accessed | tf_op | source)
XLA Modules:
  0.0 24.5 jit_solution(984159056170712949)
XLA Ops:
  0.6 22.0 %shard_map.50 = (f32[1,768]{1,0:T(1,128)}, f32[1,768]{1,0:T(1,128)}) custom-call(bf16[768,512]{1,0:T(8,128)(2,1)} %bitcast.2, bf16[1,768]{1,0:T(2,128)(2,1)} %x_ref.1, f32[32,512]{1,0:T(8,128)} %bitcast.3), custom_call_target="tpu_custom_call" | custom-call | tf_op jit(solution)/shard_map/pallas_call | solution.py:177
  22.6 0.0 copy-start.1
  22.6 0.7 %copy-done.1 = f32[1,768]{1,0:T(1,128)S(1)} copy-done((f32[1,768]{1,0:T(1,128)S(1)}, f32[1,768]{1,0:T(1,128)}, u32[]{:S(2)}) %copy-start.1) | copy-done | bytes 3096
  23.3 0.0 copy-start
  23.3 0.6 %reduce = f32[768]{0:T(1024)} reduce(f32[1,768]{1,0:T(1,128)S(1)} %copy-done.1, f32[]{:T(128)} %constant.3), dimensions={0}, to_apply=%get-tuple-element.5.reduce_sub_computation | reduce | bytes 6148 | tf_op jit(solution)/shard_map/pallas_call | solution.py:177
  23.9 0.1 copy-done
  24.0 0.6 %copy.6 = f32[1,768]{1,0:T(1,128)} copy(f32[1,768]{1,0:T(1,128)S(1)} %copy-done) | data formatting | bytes 6144
Async XLA Ops:
  22.6 0.7 %copy-start.1 = (f32[1,768]{1,0:T(1,128)S(1)}, f32[1,768]{1,0:T(1,128)}, u32[]{:S(2)}) copy-start(f32[1,768]{1,0:T(1,128)} %get-tuple-element.5) | copy-start | bytes 9220
  23.3 0.7 %copy-start = (f32[1,768]{1,0:T(1,128)S(1)}, f32[1,768]{1,0:T(1,128)}, u32[]{:S(2)}) copy-start(f32[1,768]{1,0:T(1,128)} %get-tuple-element.8) | copy-start | bytes 9220

commit v2 on v1

v2 whole, which is shorter than its diff:
```python
import functools

import jax
import jax.numpy as jnp
from jax import lax
from jax.experimental import pallas as pl
from jax.experimental.pallas import tpu as pltpu
from jax.sharding import PartitionSpec as P

MESH = pl.DeviceIdType.MESH
F32 = jnp.float32
BF16 = jnp.bfloat16


def split(value):
    high = value.astype(BF16)
    low = (value - high.astype(F32)).astype(BF16)
    return jnp.concatenate([high, low], axis=0)


def kernel(
    n, nb, chunks, s_hbm, x_hbm, c_hbm, out_ref, s_ref, x_ref, c_ref, t_ref, z_ref, a_ref, b_ref, pair_ref, mine_ref, in_ref, d_ref,
    blk_ref, load_sem, pair_send, pair_recv, go_send, go_recv, all_send, all_recv, over_send, over_recv, blk_send, blk_recv,
):
    me, group = lax.axis_index("band"), lax.axis_index("blk")
    chips = n // 2
    chip, core = me // 2, me % 2
    partner = chip * 2 + (1 - core)
    rows, width = c_ref.shape[0], c_ref.shape[1] // 2
    half = width // 2
    piece = half // chunks
    first = chips // 2 - 1
    others = [(chip + step) % chips for step in range(1, chips)]
    peers = [(group + step) % nb for step in range(1, nb)]

    barrier = pltpu.get_barrier_semaphore()
    pl.semaphore_signal(barrier, inc=1, device_id={"band": partner}, device_id_type=MESH)
    for other in others:
        pl.semaphore_signal(barrier, inc=1, device_id={"band": other * 2 + core}, device_id_type=MESH)
    for peer in peers:
        pl.semaphore_signal(barrier, inc=1, device_id={"blk": peer}, device_id_type=MESH)
    loads = [
        pltpu.make_async_copy(source, target, load_sem.at[index])
        for index, (source, target) in enumerate(((c_hbm, c_ref), (x_hbm, x_ref), (s_hbm, s_ref)))
    ]
    for load in loads:
        load.start()

    t_ref[...] = jnp.zeros_like(t_ref)
    z_ref[...] = jnp.zeros_like(z_ref)
    loads[0].wait()
    real, imag = c_ref[:, :width], c_ref[:, width:]
    within = pl.multiple_of((me % chips) * rows, rows)
    z_ref[pl.ds(within, rows), :] = (real + imag) * 0.5
    t_ref[:, pl.ds(pl.multiple_of((me // chips) * half, half), half)] = z_ref[...].T
    t_ref[pl.ds(pl.multiple_of(me * rows, rows), rows), :] += (real - imag) * 0.5
    loads[1].wait()
    x = x_ref[...].astype(F32)
    loads[2].wait()

    def build(side):
        at = pl.multiple_of(side * half, half)
        a_half = s_ref[:, pl.ds(at, half)].T
        b_half = s_ref[:, pl.ds(pl.multiple_of(width + side * half, half), half)].T
        a_ref[pl.ds(at, half), :] = a_half
        b_ref[pl.ds(at, half), :] = b_half
        a_wide, b_wide = a_half.astype(F32), b_half.astype(F32)
        total = jnp.dot(split(x * (a_wide - b_wide)), s_ref[:, :width], preferred_element_type=F32)
        total += jnp.dot(split(x * (a_wide + b_wide)), s_ref[:, width:], preferred_element_type=F32)
        return t_ref[pl.ds(at, half), :] - (total[:half] + total[half:])

    pair_ref[0] = build(1 - core).reshape(chunks, piece, width)

    pl.semaphore_wait(barrier, 1 + len(others) + len(peers))

    swaps = []
    for j in range(chunks):
        copy = pltpu.make_async_remote_copy(
            src_ref=pair_ref.at[0, j],
            dst_ref=pair_ref.at[1, j],
            send_sem=pair_send.at[j],
            recv_sem=pair_recv.at[j],
            device_id={"band": partner},
            device_id_type=MESH,
        )
        copy.start()
        swaps.append(copy)
    mine_ref[...] = build(core).reshape(mine_ref.shape)

    per = chunks // 2
    order = [(owner, owner * per + j) for j in range(per) for owner in range(2)]

    def to_owner(owner, j):
        return pltpu.make_async_remote_copy(
            src_ref=mine_ref.at[j],
            dst_ref=in_ref.at[chip, j % per],
            send_sem=go_send.at[j],
            recv_sem=go_recv.at[chip, j % per],
            device_id={"band": (first + owner) * 2 + core},
            device_id_type=MESH,
        )

    def from_chip(other, j):
        return pltpu.make_async_remote_copy(
            src_ref=mine_ref.at[j],
            dst_ref=in_ref.at[other, j % per],
            send_sem=go_send.at[j],
            recv_sem=go_recv.at[other, j % per],
            device_id={"band": other * 2 + core},
            device_id_type=MESH,
        )

    def spread(step, j):
        return pltpu.make_async_remote_copy(
            src_ref=d_ref.at[core, j],
            dst_ref=d_ref.at[core, j],
            send_sem=all_send.at[step, j],
            recv_sem=all_recv.at[j],
            device_id={"band": others[step] * 2 + core},
            device_id_type=MESH,
        )

    def hand_over(j):
        return pltpu.make_async_remote_copy(
            src_ref=d_ref.at[core, j],
            dst_ref=d_ref.at[core, j],
            send_sem=over_send.at[j],
            recv_sem=over_recv.at[j],
            device_id={"band": partner},
            device_id_type=MESH,
        )

    for owner, j in order:
        swaps[j].wait_recv()
        mine_ref[j] += pair_ref[1, j]

        @pl.when(chip != first + owner)
        def _():
            to_owner(owner, j).start()

    for owner in range(2):

        @pl.when(chip == first + owner)
        def _():
            for j in range(owner * per, owner * per + per):
                total = mine_ref[j]
                for other in others:
                    from_chip(other, j).wait_recv()
                    total += in_ref[other, j % per]
                d_ref[core, j] = total
                for step in range(chips - 1):
                    spread(step, j).start()
                hand_over(j).start()

    for owner, j in order:

        @pl.when(chip != first + owner)
        def _():
            spread(0, j).wait_recv()
            hand_over(j).start()

    def quadratic(side):
        at = pl.ds(pl.multiple_of(side * half, half), half)
        d = split(d_ref[side].reshape(half, width))
        u = jnp.dot(d, a_ref[...], preferred_element_type=F32)
        v = jnp.dot(d, b_ref[...], preferred_element_type=F32)
        u, v = u[:half] + u[half:], v[:half] + v[half:]
        a_wide, b_wide = a_ref[at, :].astype(F32), b_ref[at, :].astype(F32)
        return jnp.sum(u * (a_wide - b_wide) + v * (a_wide + b_wide), axis=0, keepdims=True)

    a_wide, b_wide = a_ref[...].astype(F32), b_ref[...].astype(F32)
    power = jnp.sum(a_wide * a_wide + b_wide * b_wide, axis=0, keepdims=True)
    residual = quadratic(core)
    for j in range(chunks):
        hand_over(j).wait_recv()
    residual = (residual + quadratic(1 - core)) / (width * width)
    updated = jnp.maximum(x + residual / (power * power / (width * width)), 0.0)
    blk_ref[group] = updated

    exchanges = []
    for step, peer in enumerate(peers):
        copy = pltpu.make_async_remote_copy(
            src_ref=blk_ref.at[group],
            dst_ref=blk_ref.at[group],
            send_sem=blk_send.at[step],
            recv_sem=blk_recv.at[step],
            device_id={"blk": peer},
            device_id_type=MESH,
        )
        copy.start()
        exchanges.append(copy)
    out_ref[0:1, :] = updated
    for copy in swaps:
        copy.wait_send()
    for owner, j in order:
        hand_over(j).wait_send()

        @pl.when(chip != first + owner)
        def _():
            to_owner(owner, j).wait_send()

        @pl.when(chip == first + owner)
        def _():
            for step in range(chips - 1):
                spread(step, j).wait_send()

    for copy in exchanges:
        copy.wait_recv()
    broad = blk_ref[0]
    for index in range(1, nb):
        broad += blk_ref[index]
    out_ref[1:2, :] = broad
    for copy in exchanges:
        copy.wait_send()


def store(both_ref, up_ref, bb_ref):
    up_ref[...] = both_ref[0:1, :]
    bb_ref[...] = both_ref[1:2, :].reshape(bb_ref.shape)


CHUNKS = 4


def body(n, nb, steering, estimates, spectra):
    points, doubled = steering.shape[1:]
    rows, width = spectra.shape[1], doubled // 2
    half, chunks = width // 2, CHUNKS
    piece = half // chunks
    dma = pltpu.SemaphoreType.DMA
    both = pl.pallas_call(
        functools.partial(kernel, n, nb, chunks),
        out_shape=jax.ShapeDtypeStruct((2, points), F32),
        in_specs=[pl.BlockSpec(memory_space=pltpu.HBM)] * 3,
        out_specs=pl.BlockSpec(memory_space=pltpu.VMEM),
        scratch_shapes=[
            pltpu.VMEM((points, doubled), BF16),
            pltpu.VMEM((1, points), BF16),
            pltpu.VMEM((rows, doubled), F32),
            pltpu.VMEM((width, width), F32),
            pltpu.VMEM((half, width), F32),
            pltpu.VMEM((width, points), BF16),
            pltpu.VMEM((width, points), BF16),
            pltpu.VMEM((2, chunks, piece, width), F32),
            pltpu.VMEM((chunks, piece, width), F32),
            pltpu.VMEM((n // 2, chunks // 2, piece, width), F32),
            pltpu.VMEM((2, chunks, piece, width), F32),
            pltpu.VMEM((nb, 1, points), F32),
            dma((3,)),
            dma((chunks,)), dma((chunks,)),
            dma((chunks,)), dma((n // 2, chunks // 2)),
            dma((n // 2 - 1, chunks)), dma((chunks,)),
            dma((chunks,)), dma((chunks,)),
            dma((nb - 1,)), dma((nb - 1,)),
        ],
        compiler_params=pltpu.CompilerParams(collective_id=0, has_side_effects=True, vmem_limit_bytes=60 * 2**20),
    )(steering[0], estimates, spectra[0])
    updated, broadband = pl.pallas_call(
        store,
        out_shape=[jax.ShapeDtypeStruct((1, points), F32), jax.ShapeDtypeStruct((points,), F32)],
        in_specs=[pl.BlockSpec(memory_space=pltpu.VMEM)],
        out_specs=[pl.BlockSpec(memory_space=pltpu.VMEM)] * 2,
        compiler_params=pltpu.CompilerParams(vmem_limit_bytes=4 * 2**20),
    )(both)
    return updated, broadband


def solution(mesh):
    return jax.shard_map(
        functools.partial(body, mesh.shape["band"], mesh.shape["blk"]),
        mesh=mesh,
        in_specs=(P("blk", "band", None), P("blk", "band"), P("blk", "band", None)),
        out_specs=(P("blk", "band"), P("band")),
        check_vma=False,
    )
```

time: 24.7 us -> 22.9 us (0.927)
  local copies, waits for them, and re-layouts: 1.3 us -> 0.68 us
  Pallas kernels: 22 us -> 21.4 us
  other arithmetic: 0.6 us -> 0 us
    unnamed x5 -> x2, local copies, waits for them, and re-layouts: 1.3 us -> 0.68 us
    pallas_call x1 -> x0, other arithmetic: 0.6 us -> none  [body(): pl.pallas_call(functools.partial(kernel, n, nb), out_shape=[jax.ShapeDtyp...]
    pallas_call x1 -> x2, Pallas kernels: 22 us -> 21.4 us  [the longest x1 20.8 us: body(): pl.pallas_call(functools.partial(kernel, n, nb, chunks), out_shape=jax.Sh...]
where the time goes in v2:
time: 22.9 us; the launch traced here: 22.8 us
  Pallas kernels  21.4 us (93%)
  local copies, waits for them, and re-layouts  0.68 us (3%)
  between operations  0.65 us (3%)
    pallas_call x1, Pallas kernels, body(): pl.pallas_call(functools.partial(kernel, n, nb, chunks), out_shape=jax.Sh...  20.8 us
    unnamed x2, local copies, waits for them, and re-layouts  0.68 us
    pallas_call x1, Pallas kernels, body(): pl.pallas_call(store, out_shape=[jax.ShapeDtypeStruct((1, points), F32),...  0.58 us

profile of v2, /device:TPU:0, one launch (start us, length us, event | category | flops | bytes accessed | tf_op | source)
XLA Modules:
  0.0 22.8 jit_solution(17377910405099137629)
XLA Ops:
  0.6 20.8 %shard_map.50.both_ref = f32[2,768]{1,0:T(2,128)} custom-call(bf16[768,512]{1,0:T(8,128)(2,1)} %bitcast.2, bf16[1,768]{1,0:T(2,128)(2,1)} %x_hbm.1, f32[32,512]{1,0:T(8,128)} %bitcast.3), custom_call_target="tpu_custom_call" | custom-call | tf_op jit(solution)/shard_map/pallas_call | solution.py:231
  21.5 0.0 copy-start
  21.5 0.7 %copy-done = f32[2,768]{1,0:T(2,128)S(1)} copy-done((f32[2,768]{1,0:T(2,128)S(1)}, f32[2,768]{1,0:T(2,128)}, u32[]{:S(2)}) %copy-start) | copy-done | bytes 6168
  22.2 0.6 %shard_map.51 = (f32[1,768]{1,0:T(1,128)}, f32[768]{0:T(1024)}) custom-call(f32[2,768]{1,0:T(2,128)S(1)} %copy-done), custom_call_target="tpu_custom_call" | custom-call | tf_op jit(solution)/shard_map/pallas_call | solution.py:258
Async XLA Ops:
  21.5 0.7 %copy-start = (f32[2,768]{1,0:T(2,128)S(1)}, f32[2,768]{1,0:T(2,128)}, u32[]{:S(2)}) copy-start(f32[2,768]{1,0:T(2,128)} %shard_map.50.both_ref) | copy-start | bytes 18436

commit v3 on v2

--- a/solution.py
+++ b/solution.py
@@ -253,7 +253,7 @@
             dma((chunks,)), dma((chunks,)),
             dma((nb - 1,)), dma((nb - 1,)),
         ],
-        compiler_params=pltpu.CompilerParams(collective_id=0, has_side_effects=True, vmem_limit_bytes=60 * 2**20),
+        compiler_params=pltpu.CompilerParams(collective_id=0, has_side_effects=True, vmem_limit_bytes=55168 * 1024),
     )(steering[0], estimates, spectra[0])
     updated, broadband = pl.pallas_call(
         store,

time: 22.9 us -> 22.3 us (0.974)
  Pallas kernels: 21.4 us -> 20.8 us
    pallas_call x1, Pallas kernels: 20.8 us -> 20.2 us  [body(): pl.pallas_call(functools.partial(kernel, n, nb, chunks), out_shape=jax.Sh...]
where the time goes in v3:
time: 22.3 us; the launch traced here: 22.1 us
  Pallas kernels  20.8 us (93%)
  local copies, waits for them, and re-layouts  0.68 us (3%)
  between operations  0.65 us (3%)
    pallas_call x1, Pallas kernels, body(): pl.pallas_call(functools.partial(kernel, n, nb, chunks), out_shape=jax.Sh...  20.2 us
    unnamed x2, local copies, waits for them, and re-layouts  0.68 us
    pallas_call x1, Pallas kernels, body(): pl.pallas_call(store, out_shape=[jax.ShapeDtypeStruct((1, points), F32),...  0.59 us

profile of v3, /device:TPU:0, one launch (start us, length us, event | category | flops | bytes accessed | tf_op | source)
XLA Modules:
  0.0 22.1 jit_solution(6691060290964109265)
XLA Ops:
  0.6 0.0 copy-start
  0.6 0.7 %copy-done = bf16[1,768]{1,0:T(2,128)(2,1)S(1)} copy-done((bf16[1,768]{1,0:T(2,128)(2,1)S(1)}, bf16[1,768]{1,0:T(2,128)(2,1)}, u32[]{:S(2)}) %copy-start) | copy-done | bytes 1560
  1.3 20.2 %shard_map.50.both_ref = f32[2,768]{1,0:T(2,128)S(1)} custom-call(bf16[768,512]{1,0:T(8,128)(2,1)} %bitcast.2, bf16[1,768]{1,0:T(2,128)(2,1)S(1)} %copy-done, f32[32,512]{1,0:T(8,128)} %bitcast.3), custom_call_target="tpu_custom_call" | custom-call | tf_op jit(solution)/shard_map/pallas_call | solution.py:231
  21.5 0.6 %shard_map.51 = (f32[1,768]{1,0:T(1,128)}, f32[768]{0:T(1024)}) custom-call(f32[2,768]{1,0:T(2,128)S(1)} %shard_map.50.both_ref), custom_call_target="tpu_custom_call" | custom-call | tf_op jit(solution)/shard_map/pallas_call | solution.py:258
Async XLA Ops:
  0.6 0.7 %copy-start = (bf16[1,768]{1,0:T(2,128)(2,1)S(1)}, bf16[1,768]{1,0:T(2,128)(2,1)}, u32[]{:S(2)}) copy-start(bf16[1,768]{1,0:T(2,128)(2,1)} %x_hbm.1) | copy-start | bytes 4612
